TPU v7x, 256 devices: a whole 4x4x8 slice. The times are simulated.
256 devices in a mesh: samp: 64 (over z, y, core), var: 4 (over x).
Axes of the slice: x: 4, y: 4, z: 8, core: 2. Of those that a mesh axis runs over, the one named last changes fastest.
Arguments:
- dosage: bfloat16 [16384, 40960], P('samp', 'var'), may hold values from 0 to 2
- centers: float32 [40960], replicated, may hold values from 0.4 to 1.34
- scales: float32 [40960], replicated, may hold values from 1.6 to 2.2
- phenotype: float32 [16384], P('samp'), may hold values from -6 to 6
- fold_ids: int32 [16384], P('samp'), may hold values from 0 to 3
- strong_blocks: int32 [32], replicated, may hold values from 0 to 319, as said below
- warm_start: float32 [4096, 32], replicated, may hold values from -4 to 4
- penalty: float32 [8], replicated, may hold values from 0.05 to 0.5
- step_size: float32 [32], replicated, may hold values from 0.2 to 0.6
Outputs:
- margin: float32 [40960], P('var')
- coefficients: float32 [4096, 32], P('var')
Inputs may be any that keep to these rules, and one draw needn't show every extreme that they name: `strong_blocks`: 32 different block numbers.
All inputs are finite; a program needn't handle non-finite values.
Results may differ from a plain program's by a relative error of at most 0.0075.
Values may be sent and summed in bfloat16 or wider, within the bound.
No kernel may reach another device: no remote copies, remote signals or barrier semaphores. Data moves between devices by JAX's collectives and lax.ppermute only.
A program may use at most 64 MiB of HBM per device.

v0:
```python
import math
import jax
import jax.numpy as jnp
from jax import lax
from jax.sharding import PartitionSpec as P

BLOCK = 128
NS = 4096
LAMBDAS = 8
FOLDS = 4
ITERS = 3
exact_mode = lax.Precision.HIGHEST


def shards(
    dosage, centers, scales, phenotype, fold_ids, strong_blocks, warm_start, penalty, step_size
):
    rows, local_width = dosage.shape
    groups = lax.axis_size("var")
    place = lax.axis_index("var")
    fit_total = LAMBDAS * FOLDS
    fit_folds = jnp.arange(fit_total, dtype=jnp.int32) % FOLDS
    weights = (fold_ids[:, None] != fit_folds[None, :]).astype(jnp.float32)
    counts = lax.psum(jnp.sum(weights, axis=0), "samp")
    fit_penalty = jnp.repeat(penalty, FOLDS)
    threshold = step_size * fit_penalty
    local_blocks = local_width // BLOCK
    relative = strong_blocks - place * local_blocks
    owned = (relative >= 0) & (relative < local_blocks)
    picked = jnp.take(
        dosage.reshape(rows, local_blocks, BLOCK), jnp.clip(relative, 0, local_blocks - 1), axis=1
    )
    masked = (picked * owned.astype(jnp.bfloat16)[None, :, None]).reshape(rows, NS)
    columns = (
        strong_blocks[:, None] * BLOCK + jnp.arange(BLOCK, dtype=jnp.int32)[None, :]
    ).reshape(NS)
    strong_centers = centers[columns]
    strong_scales = scales[columns]
    owned_columns = jnp.repeat(owned.astype(jnp.float32), BLOCK)
    share = NS // groups
    point = warm_start
    part_centers = strong_centers * owned_columns
    part_threshold = threshold[None, :]

    def residual_of(coef):
        scaled = (strong_scales[:, None] * coef).astype(jnp.bfloat16)
        partial_fit = jnp.dot(masked, scaled, preferred_element_type=jnp.float32)
        partial_fit = (
            partial_fit - jnp.dot(part_centers * strong_scales, coef, precision=exact_mode)[None, :]
        )
        fitted = lax.psum(partial_fit.astype(jnp.bfloat16), "var").astype(jnp.float32)
        return (weights * (phenotype[:, None] - fitted)).astype(jnp.bfloat16)

    rounded = residual_of(point)
    column_sums = jnp.sum(rounded.astype(jnp.float32), axis=0)
    local_centers = lax.dynamic_slice_in_dim(centers, place * local_width, local_width, 0)
    local_scales = lax.dynamic_slice_in_dim(scales, place * local_width, local_width, 0)
    cross = lax.dot_general(
        dosage, rounded, (((0,), (0,)), ((), ())), preferred_element_type=jnp.float32
    )
    total = lax.psum(cross - local_centers[:, None] * column_sums[None, :], "samp")
    margin = jnp.max(
        jnp.abs(local_scales[:, None] * total / counts[None, :]) / fit_penalty[None, :], axis=1
    )
    momentum = 1.0
    previous = point
    for sweep in range(ITERS):
        if sweep > 0:
            rounded = residual_of(point)
            column_sums = jnp.sum(rounded.astype(jnp.float32), axis=0)
        gradient_cross = lax.dot_general(
            masked, rounded, (((0,), (0,)), ((), ())), preferred_element_type=jnp.float32
        )
        gradient_cross = gradient_cross - part_centers[:, None] * column_sums[None, :]
        gradient_total = lax.psum(gradient_cross, ("samp", "var"))
        moved = point + step_size[None, :] * (
            strong_scales[:, None] * gradient_total / counts[None, :]
        )
        current = moved - jnp.clip(moved, -part_threshold, part_threshold)
        following = (1.0 + math.sqrt(1.0 + 4.0 * momentum * momentum)) / 2.0
        point = current + (momentum - 1.0) / following * (current - previous)
        previous = current
        momentum = following
    coefficients = lax.dynamic_slice_in_dim(previous, place * share, share, 0)
    return (margin, coefficients)


def solution(mesh):
    return jax.shard_map(
        shards,
        mesh=mesh,
        in_specs=(P("samp", "var"), P(), P(), P("samp"), P("samp"), P(), P(), P(), P()),
        out_specs=(P("var"), P("var", None)),
        check_vma=False,
    )
```

profile of v0, /device:TPU:2, one launch (start us, length us, event | category | flops | bytes accessed | tf_op | source)
XLA Modules:
  0.0 1087.9 jit_solution(17105678928884932665)
XLA Ops:
  7.2 7.9 copy.11
  15.2 7.9 copy.12
  23.1 3.4 gather_fusion
  26.6 2.9 copy.13
  29.8 23.0 %gather_fusion.1 = f32[4096]{0:T(1024)S(1)} fusion(f32[40960]{0:T(1024)S(1)} %copy-done.1, s32[4096]{0:T(1024)S(1)} %broadcast_clamp_fusion), kind=kCustom, calls=%fused_computation.1 | custom fusion | bytes 49152 | tf_op jit(solution)/shard_map/gather | solution.py:38
  52.9 23.0 %gather_fusion.2 = f32[4096]{0:T(1024)S(1)} fusion(f32[40960]{0:T(1024)S(1)} %copy-done, s32[4096]{0:T(1024)S(1)} %broadcast_clamp_fusion), kind=kCustom, calls=%fused_computation.2 | custom fusion | bytes 49152 | tf_op jit(solution)/shard_map/gather | solution.py:37
  76.0 0.5 convolution_bitcast_fusion.3
  76.5 3.2 fusion.1
  79.7 0.4 fusion.3
  80.2 15.3 %psum.56 = bf16[256,32]{0,1:T(8,128)(2,1)S(1)} all-reduce(bf16[256,32]{0,1:T(8,128)(2,1)S(1)} %fusion.3), channel_id=1, replica_groups=mesh['samp'=64,'var'=4] {'var'}, use_global_device_ids=true, to_apply=%region_0.1 | all-reduce | flops 8192 | bytes 32768 | tf_op jit(solution)/shard_map/psum | solution.py:51
  95.5 0.2 fusion.11
  95.7 1.5 convolution_subtract_fusion.2
  97.4 127.1 %psum.58 = f32[32]{0:T(128)S(1)} all-reduce(f32[32]{0:T(128)S(1)} %get-tuple-element.2), channel_id=1, replica_groups=mesh['samp'=64,'var'=4] {'samp'}, use_global_device_ids=true, to_apply=%region_4.5 | all-reduce | flops 32 | bytes 256 | tf_op jit(solution)/shard_map/psum | solution.py:24
  224.5 131.6 %all-reduce.7.cloned.1.call-done = f32[4096,32]{0,1:T(8,128)} async-done(((f32[4096,32]{0,1:T(8,128)}), f32[4096,32]{0,1:T(8,128)}) %all-reduce.7.cloned.1.call-update) | async-done | bytes 524304 | tf_op jit(solution)/shard_map/psum | solution.py:75
  356.1 1.8 convolution_bitcast_fusion.2
  357.9 0.5 fusion.4
  358.5 14.0 %psum.60 = bf16[256,32]{0,1:T(8,128)(2,1)S(1)} all-reduce(bf16[256,32]{0,1:T(8,128)(2,1)S(1)} %fusion.4), channel_id=1, replica_groups=mesh['samp'=64,'var'=4] {'var'}, use_global_device_ids=true, to_apply=%region_7.8 | all-reduce | flops 8192 | bytes 32768 | tf_op jit(solution)/shard_map/psum | solution.py:51
  372.5 0.2 convert_reduce_fusion.1
  372.7 1.5 convolution_subtract_fusion.1
  374.3 4.6 fusion
  379.0 250.2 %all-reduce.9.cloned.1.call-done = f32[4096,32]{0,1:T(8,128)} async-done(((f32[4096,32]{0,1:T(8,128)}), f32[4096,32]{0,1:T(8,128)}) %all-reduce.9.cloned.1.call-update) | async-done | bytes 524304 | tf_op jit(solution)/shard_map/psum | solution.py:75
  629.3 1.6 multiply_add_fusion
  630.9 0.5 convolution_bitcast_fusion.1
  631.4 0.4 fusion.5
  631.9 13.9 %psum.62 = bf16[256,32]{0,1:T(8,128)(2,1)S(1)} all-reduce(bf16[256,32]{0,1:T(8,128)(2,1)S(1)} %fusion.5), channel_id=1, replica_groups=mesh['samp'=64,'var'=4] {'var'}, use_global_device_ids=true, to_apply=%region_10.11 | all-reduce | flops 8192 | bytes 32768 | tf_op jit(solution)/shard_map/psum | solution.py:51
  645.8 0.2 convert_reduce_fusion
  646.0 1.5 convolution_subtract_fusion
  647.5 172.9 %all-reduce.5.cloned.1.call-done = f32[10240,32]{0,1:T(8,128)} async-done(((f32[10240,32]{0,1:T(8,128)}), f32[10240,32]{0,1:T(8,128)}) %all-reduce.5.cloned.1.call-update) | async-done | bytes 1310736 | tf_op jit(solution)/shard_map/psum | solution.py:61
  820.4 2.3 fusion.2
  822.7 256.9 %all-reduce.11.cloned.1.call-done = f32[4096,32]{0,1:T(8,128)} async-done(((f32[4096,32]{0,1:T(8,128)}), f32[4096,32]{0,1:T(8,128)}) %all-reduce.11.cloned.1.call-update) | async-done | bytes 524304 | tf_op jit(solution)/shard_map/psum | solution.py:75
  1079.6 1.1 broadcast_multiply_fusion
  1080.6 0.8 minimum_subtract_fusion.1
  (48 shorter events, 0.8 us)
Async XLA Ops:
  7.2 348.9 %all-reduce.7.cloned.1.call-start = ((), (), s32[]{:S(2)}) async-start(), calls=%async_computation.1 | async-start | bytes 1048576 | tf_op jit(solution)/shard_map/psum | solution.py:75
  15.2 7.9 copy-start.10
  26.6 3.2 copy-start.1
  29.8 23.1 %copy-start = (f32[40960]{0:T(1024)S(1)}, f32[40960]{0:T(1024)}, u32[]{:S(2)}) copy-start(f32[40960]{0:T(1024)} %param.10) | copy-start | bytes 491524
  52.8 23.1 %copy-start.2 = (f32[4096,32]{0,1:T(8,128)S(1)}, f32[4096,32]{0,1:T(8,128)}, u32[]{:S(2)}) copy-start(f32[4096,32]{0,1:T(8,128)} %param.15) | copy-start | bytes 1572868
  79.7 15.8 %copy-start.4 = (s32[256]{0:T(256)S(1)}, s32[256]{0:T(256)}, u32[]{:S(2)}) copy-start(s32[256]{0:T(256)} %param.13) | copy-start | bytes 3076
  79.7 15.8 %copy-start.5 = (f32[256]{0:T(256)S(1)}, f32[256]{0:T(256)}, u32[]{:S(2)}) copy-start(f32[256]{0:T(256)} %param.12) | copy-start | bytes 3076
  80.1 17.1 %copy-start.9 = (f32[8]{0:T(128)S(1)}, f32[8]{0:T(128)}, u32[]{:S(2)}) copy-start(f32[8]{0:T(128)} %param.16) | copy-start | bytes 100
  80.2 144.4 %copy-start.6 = (f32[32]{0:T(128)S(1)}, f32[32]{0:T(128)}, u32[]{:S(2)}) copy-start(f32[32]{0:T(128)} %param.17) | copy-start | bytes 388
  95.7 128.9 %copy-start.7 = (f32[32]{0:T(128)}, f32[32]{0:T(128)S(1)}, u32[]{:S(2)}) copy-start(f32[32]{0:T(128)S(1)} %get-tuple-element.3) | copy-start | bytes 388
  97.2 532.1 %all-reduce.9.cloned.1.call-start = ((), (), s32[]{:S(2)}) async-start(), calls=%async_computation.2 | async-start | bytes 1048576 | tf_op jit(solution)/shard_map/psum | solution.py:75
  356.1 1.8 copy-start.3
  358.5 15.9 %dynamic-slice-start = ((f32[40960]{0:T(1024)}, s32[]{:T(128)}), f32[10240]{0:T(1024)S(1)}, s32[]{:S(2)}) async-start(f32[40960]{0:T(1024)} %param.10, s32[]{:T(128)} %select_n.39), calls=%async_computation.4 | async-start | bytes 82432 | tf_op jit(solution)/shard_map/dynamic_slice | solution.py:56
  358.5 15.9 %copy-start.8 = (f32[32]{0:T(128)S(1)}, f32[32]{0:T(128)}, u32[]{:S(2)}) copy-start(f32[32]{0:T(128)} %copy-done.7) | copy-start | bytes 388
  374.3 446.2 %all-reduce.5.cloned.1.call-start = ((), (), s32[]{:S(2)}) async-start(), calls=%async_computation | async-start | bytes 2621440 | tf_op jit(solution)/shard_map/psum | solution.py:61
  379.0 700.6 %all-reduce.11.cloned.1.call-start = ((), (), s32[]{:S(2)}) async-start(), calls=%async_computation.3 | async-start | bytes 1048576 | tf_op jit(solution)/shard_map/psum | solution.py:75
  631.9 188.6 %dynamic-slice-start.1 = ((f32[40960]{0:T(1024)}, s32[]{:T(128)}), f32[10240]{0:T(1024)S(1)}, s32[]{:S(2)}) async-start(f32[40960]{0:T(1024)} %param.11, s32[]{:T(128)} %select_n.39), calls=%async_computation.5 | async-start | bytes 82432 | tf_op jit(solution)/shard_map/dynamic_slice | solution.py:57
Sparse Core Ops, SparseCore 0:
  97.3 258.7 all-reduce.6
  374.4 254.8 all-reduce.8
  632.7 187.6 all-reduce.4
  825.7 253.7 all-reduce.10
where the time goes:
time: 1090 us
  waiting for transfers between devices  812 us (74%)
  blocking collectives  170 us (16%)
  local copies, waits for them, and re-layouts  68.7 us (6%)
  between operations  14 us (1%)
  matrix products  13.4 us (1%)
    psum x3, waiting for transfers between devices, shards(): gradient_total = lax.psum(gradient_cross, ('samp', 'var'))  639 us
    psum x1, waiting for transfers between devices, shards(): lax.psum(cross - local_centers[:, None] * column_sums[None, :], 'samp')  173 us
    psum x1, blocking collectives, shards(): counts = lax.psum(jnp.sum(weights, axis=0), 'samp')  127 us
    psum x3, blocking collectives, residual_of(): lax.psum(partial_fit.astype(jnp.bfloat16), 'var').astype(jnp.float32)  43.3 us
    gather x1, local copies, waits for them, and re-layouts, shards(): strong_scales = scales[columns]  23 us
    gather x1, local copies, waits for them, and re-layouts, shards(): strong_centers = centers[columns]  23 us
  transfers between devices with their start and end apart: 4, of which 4 were waited for; matrix products, arithmetic and copies ran while one was open for 1% of the time, Pallas kernels for 0%

commit v1 on v0

--- a/solution.py
+++ b/solution.py
@@ -72,7 +72,7 @@
             masked, rounded, (((0,), (0,)), ((), ())), preferred_element_type=jnp.float32
         )
         gradient_cross = gradient_cross - part_centers[:, None] * column_sums[None, :]
-        gradient_total = lax.psum(gradient_cross, ("samp", "var"))
+        gradient_total = lax.psum(lax.psum(gradient_cross, "samp"), "var")
         moved = point + step_size[None, :] * (
             strong_scales[:, None] * gradient_total / counts[None, :]
         )

time: 1090 us -> 925 us (0.85)
  waiting for transfers between devices: 812 us -> 646 us
    psum x3 -> x5, waiting for transfers between devices: 639 us -> 454 us  [shards(): gradient_total = lax.psum(lax.psum(gradient_cross, 'samp'), 'var')]
    psum x1, waiting for transfers between devices: 173 us -> 192 us  [shards(): lax.psum(cross - local_centers[:, None] * column_sums[None, :], 'samp')]
  transfers between devices with their start and end apart: 4 -> 6, of which waited for: 4 -> 5; matrix products, arithmetic and copies ran while one was open for 1% -> 1% of each run, Pallas kernels for 0% -> 0%
where the time goes in v1:
time: 925 us; the launch traced here: 923 us
  waiting for transfers between devices  646 us (70%)
  blocking collectives  170 us (18%)
  local copies, waits for them, and re-layouts  68.7 us (7%)
  matrix products  14.6 us (2%)
  between operations  14.4 us (2%)
  other arithmetic  10.2 us (1%)
    psum x5, waiting for transfers between devices, shards(): gradient_total = lax.psum(lax.psum(gradient_cross, 'samp'), 'var')  454 us
    psum x1, waiting for transfers between devices, shards(): lax.psum(cross - local_centers[:, None] * column_sums[None, :], 'samp')  192 us
    psum x1, blocking collectives, shards(): counts = lax.psum(jnp.sum(weights, axis=0), 'samp')  125 us
    psum x3, blocking collectives, residual_of(): lax.psum(partial_fit.astype(jnp.bfloat16), 'var').astype(jnp.float32)  44.5 us
    gather x1, local copies, waits for them, and re-layouts, shards(): strong_scales = scales[columns]  23 us
    gather x1, local copies, waits for them, and re-layouts, shards(): strong_centers = centers[columns]  23 us
  transfers between devices with their start and end apart: 6, of which 5 were waited for; matrix products, arithmetic and copies ran while one was open for 1% of the time, Pallas kernels for 0%

profile of v1, /device:TPU:2, one launch (start us, length us, event | category | flops | bytes accessed | tf_op | source)
XLA Modules:
  0.0 923.5 jit_solution(15734939986361196987)
XLA Ops:
  7.2 7.9 copy.11
  15.2 7.9 copy.12
  23.1 3.4 gather_fusion
  26.6 2.9 copy.13
  29.8 23.0 %gather_fusion.1 = f32[4096]{0:T(1024)S(1)} fusion(f32[40960]{0:T(1024)S(1)} %copy-done.1, s32[4096]{0:T(1024)S(1)} %broadcast_clamp_fusion), kind=kCustom, calls=%fused_computation.1 | custom fusion | bytes 49152 | tf_op jit(solution)/shard_map/gather | solution.py:38
  52.9 23.0 %gather_fusion.2 = f32[4096]{0:T(1024)S(1)} fusion(f32[40960]{0:T(1024)S(1)} %copy-done, s32[4096]{0:T(1024)S(1)} %broadcast_clamp_fusion), kind=kCustom, calls=%fused_computation.2 | custom fusion | bytes 49152 | tf_op jit(solution)/shard_map/gather | solution.py:37
  76.0 0.5 convolution_bitcast_fusion.3
  76.5 3.2 fusion.1
  79.7 0.4 fusion.3
  80.2 15.3 %psum.77 = bf16[256,32]{0,1:T(8,128)(2,1)S(1)} all-reduce(bf16[256,32]{0,1:T(8,128)(2,1)S(1)} %fusion.3), channel_id=1, replica_groups=mesh['samp'=64,'var'=4] {'var'}, use_global_device_ids=true, to_apply=%region_0.1 | all-reduce | flops 8192 | bytes 32768 | tf_op jit(solution)/shard_map/psum | solution.py:51
  95.7 1.5 convolution_subtract_fusion.2
  97.3 186.0 %all-reduce.8.cloned.1.call-done = f32[4096,32]{0,1:T(8,128)} async-done(((f32[4096,32]{0,1:T(8,128)}), f32[4096,32]{0,1:T(8,128)}) %all-reduce.8.cloned.1.call-update) | async-done | bytes 524304 | tf_op jit(solution)/shard_map/psum | solution.py:75
  283.6 125.2 %psum.79 = f32[32]{0:T(128)S(1)} all-reduce(f32[32]{0:T(128)S(1)} %get-tuple-element.2), channel_id=1, replica_groups=mesh['samp'=64,'var'=4] {'samp'}, use_global_device_ids=true, to_apply=%region_4.5 | all-reduce | flops 32 | bytes 256 | tf_op jit(solution)/shard_map/psum | solution.py:24
  408.7 0.6 fusion.22
  409.3 1.8 convolution_bitcast_fusion.2
  411.2 1.8 fusion.4
  412.9 14.7 %psum.82 = bf16[256,32]{0,1:T(8,128)(2,1)S(1)} all-reduce(bf16[256,32]{0,1:T(8,128)(2,1)} %fusion.4), channel_id=1, replica_groups=mesh['samp'=64,'var'=4] {'var'}, use_global_device_ids=true, to_apply=%region_8.9 | all-reduce | flops 8192 | bytes 32768 | tf_op jit(solution)/shard_map/psum | solution.py:51
  427.8 1.5 convolution_subtract_fusion.1
  429.4 182.2 %all-reduce.12.cloned.1.call-done = f32[4096,32]{0,1:T(8,128)} async-done(((f32[4096,32]{0,1:T(8,128)}), f32[4096,32]{0,1:T(8,128)}) %all-reduce.12.cloned.1.call-update) | async-done | bytes 524304 | tf_op jit(solution)/shard_map/psum | solution.py:75
  611.7 4.6 fusion
  616.4 41.6 %all-reduce.14.cloned.1.call-done = f32[4096,32]{0,1:T(8,128)} async-done(((f32[4096,32]{0,1:T(8,128)}), f32[4096,32]{0,1:T(8,128)}) %all-reduce.14.cloned.1.call-update) | async-done | bytes 524304 | tf_op jit(solution)/shard_map/psum | solution.py:75
  658.0 1.6 multiply_add_fusion
  659.6 0.5 convolution_bitcast_fusion.1
  660.1 0.4 fusion.5
  660.5 14.5 %psum.85 = bf16[256,32]{0,1:T(8,128)(2,1)S(1)} all-reduce(bf16[256,32]{0,1:T(8,128)(2,1)S(1)} %fusion.5), channel_id=1, replica_groups=mesh['samp'=64,'var'=4] {'var'}, use_global_device_ids=true, to_apply=%region_12.13 | all-reduce | flops 8192 | bytes 32768 | tf_op jit(solution)/shard_map/psum | solution.py:51
  675.0 0.2 convert_reduce_fusion
  675.2 1.5 convolution_subtract_fusion
  676.8 191.6 %all-reduce.18.cloned.1.call-done = (f32[10240,32]{0,1:T(8,128)}, f32[4096,32]{0,1:T(8,128)}) async-done(((f32[10240,32]{0,1:T(8,128)}, f32[4096,32]{0,1:T(8,128)}), (f32[10240,32]{0,1:T(8,128)}, f32[4096,32]{0,1:T(8,128)})) %all-reduce.18.cloned.1.call-update) | async-done | bytes 1835024 | tf_op jit(solution)/shard_map/psum | solution.py:61
  868.5 2.3 fusion.2
  870.7 44.0 %all-reduce.16.cloned.1.call-done = f32[4096,32]{0,1:T(8,128)} async-done(((f32[4096,32]{0,1:T(8,128)}), f32[4096,32]{0,1:T(8,128)}) %all-reduce.16.cloned.1.call-update) | async-done | bytes 524304 | tf_op jit(solution)/shard_map/psum | solution.py:75
  914.8 1.1 broadcast_multiply_fusion
  915.8 0.8 minimum_subtract_fusion.1
  (67 shorter events, 1.3 us)
Async XLA Ops:
  7.2 276.2 %all-reduce.8.cloned.1.call-start = ((), (), s32[]{:S(2)}) async-start(), calls=%async_computation | async-start | bytes 1048576 | tf_op jit(solution)/shard_map/psum | solution.py:75
  15.2 7.9 copy-start.17
  26.6 3.2 copy-start.1
  29.8 23.1 %copy-start = (f32[40960]{0:T(1024)S(1)}, f32[40960]{0:T(1024)}, u32[]{:S(2)}) copy-start(f32[40960]{0:T(1024)} %param.10) | copy-start | bytes 491524
  52.8 23.1 %copy-start.2 = (f32[4096,32]{0,1:T(8,128)S(1)}, f32[4096,32]{0,1:T(8,128)}, u32[]{:S(2)}) copy-start(f32[4096,32]{0,1:T(8,128)} %param.15) | copy-start | bytes 1572868
  79.7 15.8 %copy-start.4 = (s32[256]{0:T(256)S(1)}, s32[256]{0:T(256)}, u32[]{:S(2)}) copy-start(s32[256]{0:T(256)} %param.13) | copy-start | bytes 3076
  79.7 15.8 %copy-start.5 = (f32[256]{0:T(256)S(1)}, f32[256]{0:T(256)}, u32[]{:S(2)}) copy-start(f32[256]{0:T(256)} %param.12) | copy-start | bytes 3076
  80.1 203.3 %copy-start.16 = (f32[8]{0:T(128)S(1)}, f32[8]{0:T(128)}, u32[]{:S(2)}) copy-start(f32[8]{0:T(128)} %param.16) | copy-start | bytes 100
  80.2 328.6 %copy-start.6 = (f32[32]{0:T(128)S(1)}, f32[32]{0:T(128)}, u32[]{:S(2)}) copy-start(f32[32]{0:T(128)} %param.17) | copy-start | bytes 388
  95.7 187.7 %copy-start.14 = (f32[32]{0:T(128)}, f32[32]{0:T(128)S(1)}, u32[]{:S(2)}) copy-start(f32[32]{0:T(128)S(1)} %get-tuple-element.3) | copy-start | bytes 388
  97.2 312.1 %all-reduce.10.cloned.1.call-start = ((), (), s32[]{:S(2)}) async-start(), calls=%async_computation.1 | async-start | bytes 1048576 | tf_op jit(solution)/shard_map/psum | solution.py:75
  283.4 328.3 %all-reduce.12.cloned.1.call-start = ((), (), s32[]{:S(2)}) async-start(), calls=%async_computation.2 | async-start | bytes 1048576 | tf_op jit(solution)/shard_map/psum | solution.py:75
  283.6 125.7 %copy-start.12 = (f32[32]{0:T(128)}, f32[32]{0:T(128)S(1)}, u32[]{:S(2)}) copy-start(f32[32]{0:T(128)S(1)} %div.40) | copy-start | bytes 388
  409.3 1.8 copy-start.3
  409.3 1.8 copy-start.8
  409.3 1.8 copy-start.10
  412.9 198.8 %copy-start.15 = (f32[32]{0:T(128)S(1)}, f32[32]{0:T(128)}, u32[]{:S(2)}) copy-start(f32[32]{0:T(128)} %copy-done.14) | copy-start | bytes 388
  429.4 228.6 %all-reduce.14.cloned.1.call-start = ((), (), s32[]{:S(2)}) async-start(), calls=%async_computation.3 | async-start | bytes 1048576 | tf_op jit(solution)/shard_map/psum | solution.py:75
  611.6 256.8 %all-reduce.18.cloned.1.call-start = ((), (), s32[]{:S(2)}) async-start(), calls=%async_computation.5 | async-start | bytes 3670016 | tf_op jit(solution)/shard_map/psum | solution.py:61
  611.7 46.3 %copy-start.7 = (f32[32]{0:T(128)S(1)}, f32[32]{0:T(128)}, u32[]{:S(2)}) copy-start(f32[32]{0:T(128)} %param.17) | copy-start | bytes 388
  611.7 46.2 %copy-start.9 = (f32[32]{0:T(128)S(1)}, f32[32]{0:T(128)}, u32[]{:S(2)}) copy-start(f32[32]{0:T(128)} %get-tuple-element.6) | copy-start | bytes 388
  611.7 46.2 %copy-start.11 = (f32[32]{0:T(128)S(1)}, f32[32]{0:T(128)}, u32[]{:S(2)}) copy-start(f32[32]{0:T(128)} %get-tuple-element.7) | copy-start | bytes 388
  675.2 193.3 %dynamic-slice-start = ((f32[40960]{0:T(1024)}, s32[]{:T(128)}), f32[10240]{0:T(1024)S(1)}, s32[]{:S(2)}) async-start(f32[40960]{0:T(1024)} %param.11, s32[]{:T(128)} %select_n.39), calls=%async_computation.6 | async-start | bytes 82432 | tf_op jit(solution)/shard_map/dynamic_slice | solution.py:57
  675.2 193.3 %copy-start.13 = (f32[32]{0:T(128)S(1)}, f32[32]{0:T(128)}, u32[]{:S(2)}) copy-start(f32[32]{0:T(128)} %copy-done.12) | copy-start | bytes 388
  676.8 238.0 %all-reduce.16.cloned.1.call-start = ((), (), s32[]{:S(2)}) async-start(), calls=%async_computation.4 | async-start | bytes 1048576 | tf_op jit(solution)/shard_map/psum | solution.py:75
Sparse Core Ops, SparseCore 0:
  97.4 185.9 all-reduce.7
  285.7 44.2 all-reduce.9
  429.5 182.0 all-reduce.11
  613.8 44.1 all-reduce.13
  676.9 191.5 all-reduce.17
  870.6 44.0 all-reduce.15
